TPU v7x, 32 devices: a whole 2x2x4 slice. The times are simulated.
32 devices in a mesh: tile: 8 (over y, x, core), member: 4 (over z).
Axes of the slice: x: 2, y: 2, z: 4, core: 2. Of those that a mesh axis runs over, the one named last changes fastest.
Arguments:
- hx: bfloat16 [512, 32768], P('member', 'tile'), may hold values from -6 to 6
- obs_value: bfloat16 [32768], P('tile'), may hold values from -8 to 8
- obs_rinv: bfloat16 [32768], P('tile'), may hold values from 0.29882812 to 4
- obs_index: int32 [32, 1024], P('tile'), may hold values from 512 to 5631, as said below
- loc_weight: float32 [32, 1024], P(('tile', 'member')), may hold values from 0.05 to 1
- state: bfloat16 [512, 131072], P('member', 'tile'), may hold values from -6 to 6
Outputs:
- analysis: bfloat16 [512, 131072], P('member', 'tile')
Inputs may be any that keep to these rules, and one draw needn't show every extreme that they name: `obs_index`: row p lists 1024 distinct positions in the pool of tile p // 4: positions 0 .. 1023 are the last 1024 observations of the tile before it, the next 4096 the tile's own, the last 1024 the first observations of the tile after it; the tiles form a closed band. All positions of a row lie within 2048 consecutive positions.
All inputs are finite; a program needn't handle non-finite values.
Results may differ from a plain program's by a relative error of at most 0.012.
The roundings to bfloat16 on the way count: a program that leaves them out, or rounds other values in their place, can miss the bound.
Values may be sent and summed in bfloat16 or wider, within the bound.
No kernel may reach another device: no remote copies, remote signals or barrier semaphores. Data moves between devices by JAX's collectives and lax.ppermute only.
A program may use at most 64 MiB of HBM per device.

v0:
```python
import jax
import jax.numpy as jnp
from jax import lax
from jax.sharding import PartitionSpec as P

LOC = 1024
NS_ITERS = 3


def with_halo(block, sides, width):
    for axis, dim in sides:
        count = lax.axis_size(axis)
        forward = [(i, i + 1) for i in range(count - 1)]
        forward.append((count - 1, 0))
        backward = [(target, source) for source, target in forward]
        low = lax.ppermute(
            lax.slice_in_dim(block, block.shape[dim] - width, None, axis=dim), axis, forward
        )
        high = lax.ppermute(lax.slice_in_dim(block, 0, width, axis=dim), axis, backward)
        block = jnp.concatenate([low, block, high], axis=dim)
    return block


def product_f32(left, right, dims):
    return lax.dot_general(
        left.astype(jnp.float32),
        right.astype(jnp.float32),
        (dims, ((), ())),
        precision=lax.Precision.HIGHEST,
        preferred_element_type=jnp.float32,
    )


def analysis(obs_block, obs_pair, loc_row):
    members = obs_block.shape[0]
    block_f = obs_block.astype(jnp.float32)
    obs_mean = jnp.mean(block_f, axis=0)
    obs_root = jnp.sqrt(obs_pair[1].astype(jnp.float32) * loc_row)
    scaled = ((block_f - obs_mean) * obs_root).astype(jnp.bfloat16)
    innovation = (obs_pair[0].astype(jnp.float32) - obs_mean) * obs_root
    gram_matrix = product_f32(scaled, scaled, ((1,), (1,)))
    identity = jnp.eye(members, dtype=jnp.float32)
    system = gram_matrix + (members - 1.0) * identity
    projection = jnp.dot(scaled.astype(jnp.float32), innovation, precision=lax.Precision.HIGHEST)
    norm_a = jnp.sqrt(jnp.sum(system * system))
    upper_iter = system / norm_a
    lower_iter = identity
    for sweep in range(NS_ITERS):
        upper_b = upper_iter.astype(jnp.bfloat16)
        lower_b = lower_iter.astype(jnp.bfloat16)
        product = product_f32(lower_b, upper_b, ((1,), (0,)))
        half_step = (1.5 * identity - 0.5 * product).astype(jnp.bfloat16)
        if sweep + 1 < NS_ITERS:
            upper_iter = product_f32(upper_b, half_step, ((1,), (0,)))
        lower_iter = product_f32(half_step, lower_b, ((1,), (0,)))
    invroot = lower_iter / jnp.sqrt(norm_a)
    inner_w = jnp.dot(invroot, projection, precision=lax.Precision.HIGHEST)
    mean_w = jnp.dot(invroot, inner_w, precision=lax.Precision.HIGHEST)
    transform = jnp.sqrt(members - 1.0) * invroot + mean_w[:, None]
    return transform.astype(jnp.bfloat16)


def transform_state(transform, state_block):
    block_f = state_block.astype(jnp.float32)
    state_mean = jnp.mean(block_f, axis=0)
    state_pert = (block_f - state_mean).astype(jnp.bfloat16)
    combined = product_f32(transform, state_pert, ((0,), (0,)))
    return (state_mean + combined).astype(jnp.bfloat16)


def on_device(hx, obs_value, obs_rinv, obs_index, loc_weight, state):
    ens_dev = hx.shape[0]
    member_pos = lax.axis_index("member")
    stacked = jnp.concatenate([hx, obs_value[None, :], obs_rinv[None, :]], axis=0)
    obs_pool = with_halo(stacked, (("tile", 1),), LOC)
    own_index = lax.dynamic_index_in_dim(obs_index, member_pos, 0, keepdims=False)
    obs_pair = jnp.take(obs_pool[ens_dev:], own_index, axis=1)
    picked = jnp.take(obs_pool[:ens_dev], obs_index, axis=1)
    received = lax.all_to_all(picked, "member", split_axis=1, concat_axis=0, tiled=True)
    obs_block = received[:, 0, :]
    transform = analysis(obs_block, obs_pair, loc_weight[0])
    group_count = obs_index.shape[0]
    state_split = state.reshape(ens_dev, group_count, state.shape[1] // group_count)
    updated = transform_state(
        transform,
        lax.all_to_all(state_split, "member", split_axis=1, concat_axis=0, tiled=True)[:, 0, :],
    )
    result = lax.all_to_all(updated[:, None, :], "member", split_axis=0, concat_axis=1, tiled=True)
    return result.reshape(ens_dev, state.shape[1])


def solution(mesh):
    in_specs = (
        P("member", "tile"),
        P("tile"),
        P("tile"),
        P("tile", None),
        P(("tile", "member"), None),
        P("member", "tile"),
    )
    out_specs = P("member", "tile")
    return jax.shard_map(
        on_device, mesh=mesh, in_specs=in_specs, out_specs=out_specs, check_vma=False
    )
```

profile of v0, /device:TPU:0, one launch (start us, length us, event | category | flops | bytes accessed | tf_op | source)
XLA Modules:
  0.0 328.8 jit_solution(2803960686868438312)
XLA Ops:
  0.0 1.6 copy.52
  5.1 2.9 collective-permute-start.1
  8.1 9.8 %collective-permute-done = bf16[130,1024]{0,1:T(8,128)(2,1)S(1)} collective-permute-done((bf16[130,1024]{0,1:T(8,128)(2,1)S(1)}, bf16[130,1024]{0,1:T(8,128)(2,1)S(1)}, u32[]{:S(2)}, u32[]{:S(2)}) %collective-permute-start) | collective-permute-done | bytes 266272 | tf_op jit(solution)/shard_map/ppermute | solution.py:16
  17.9 1.5 collective-permute-done.1
  19.3 10.2 %pad_maximum_fusion = bf16[130,6144]{0,1:T(8,128)(2,1)S(1)} fusion(bf16[130,1024]{0,1:T(8,128)(2,1)S(1)} %collective-permute-done.1, bf16[1,4096]{0,1:T(8,128)(2,1)S(1)} %broadcast_in_dim.45, bf16[1,4096]{0,1:T(8,128)(2,1)S(1)} %broadcast_in_dim.44, bf16[128,4096]{0,1:T(8,128)(2,1)S(1)} %copy.52, bf16[130,1024]{0,1:T(8,128)(2,1)S(1)} %collective-permute-done), kind=kLoop, calls=%fused_computation.7 | loop fusion | flops 7987200 | bytes 3194880 | tf_op jit(solution)/shard_map/concatenate | solution.py:20
  29.5 1.7 copy-done
  31.3 12.1 %gather_fusion = bf16[4096,128]{1,0:T(8,128)(2,1)S(1)} fusion(bf16[128,6144]{0,1:T(8,128)(2,1)S(1)} %slice.28, s32[4096]{0:T(1024)S(1)} %bitcast_clamp_fusion), kind=kCustom, calls=%fused_computation | custom fusion | bytes 2113536 | tf_op jit(solution)/shard_map/jit(_take)/gather | solution.py:78
  45.1 4.9 %all-to-all-start.1 = ((bf16[128,4,1024]{2,0,1:T(8,128)(2,1)}), bf16[128,4,1024]{2,0,1:T(8,128)(2,1)S(1)}, u32[]{:S(2)}, u32[]{:S(2)}) async-start(bf16[128,4,1024]{2,0,1:T(8,128)(2,1)} %select_bitcast_fusion), calls=%async_computation.1 | async-start | bytes 2097152 | tf_op jit(solution)/shard_map/all_to_all | solution.py:79
  50.0 4.7 %copy.65 = bf16[16,4,8,4096]{3,2,0,1:T(8,128)(2,1)} copy(bf16[16,4,8,4096]{3,2,1,0:T(8,128)(2,1)} %bitcast.79) | data formatting | bytes 8388608 | tf_op jit(solution)/shard_map/reshape | solution.py:83
  54.7 22.0 %all-to-all-done.1 = bf16[128,4,1024]{2,0,1:T(8,128)(2,1)S(1)} async-done(((bf16[128,4,1024]{2,0,1:T(8,128)(2,1)}), bf16[128,4,1024]{2,0,1:T(8,128)(2,1)S(1)}, u32[]{:S(2)}, u32[]{:S(2)}) %all-to-all-start.1) | async-done | bytes 1048608 | tf_op jit(solution)/shard_map/all_to_all | solution.py:79
  76.7 5.2 %all-to-all-start = ((bf16[128,4,4096]{2,0,1:T(8,128)(2,1)}), bf16[128,4,4096]{2,0,1:T(8,128)(2,1)}, u32[]{:S(2)}, u32[]{:S(2)}) async-start(bf16[128,4,4096]{2,0,1:T(8,128)(2,1)} %bitcast.76), calls=%async_computation | async-start | bytes 8388608 | tf_op jit(solution)/shard_map/all_to_all | solution.py:86
  81.9 3.2 gather_fusion.1
  85.8 1.5 multiply_reduce_fusion
  94.4 81.2 %all-to-all-done = bf16[128,4,4096]{2,0,1:T(8,128)(2,1)} async-done(((bf16[128,4,4096]{2,0,1:T(8,128)(2,1)}), bf16[128,4,4096]{2,0,1:T(8,128)(2,1)}, u32[]{:S(2)}, u32[]{:S(2)}) %all-to-all-start) | async-done | bytes 4194336 | tf_op jit(solution)/shard_map/all_to_all | solution.py:86
  175.6 3.2 convert_reduce_fusion.1
  178.8 3.1 fusion
  181.8 4.6 %fusion.1 = bf16[512,1,4096]{2,0,1:T(8,128)(2,1)} fusion(bf16[512,4096]{1,0:T(8,128)(2,1)S(1)} %fusion, f32[4096]{0:T(1024)S(1)} %broadcast_multiply_fusion, f32[512,512]{1,0:T(8,128)S(1)} %convolution_divide_fusion, f32[512]{0:T(512)S(1)} %bitcast.82), kind=kOutput, calls=%fused_computation.5 | convolution fusion | flops 2152464384 | bytes 9455616 | tf_op jit(solution)/shard_map/dot_general | solution.py:25
  186.9 6.6 %reduce.6 = bf16[512,4096]{1,0:T(8,128)(2,1)} reduce(bf16[512,1,4096]{2,0,1:T(8,128)(2,1)} %fusion.1, bf16[]{:T(256)} %broadcast.126), dimensions={1}, to_apply=%copy.57.reduce_sub_computation | reduce | bytes 8388610 | tf_op jit(solution)/shard_map/broadcast_in_dim | solution.py:88
  193.5 6.2 %reshape.136 = bf16[4,2,262144]{2,1,0:T(2,128)(2,1)} reshape(bf16[512,4096]{1,0:T(8,128)(2,1)} %reduce.6) | data formatting | bytes 8388608
  199.7 98.7 %all_to_all.33 = bf16[4,2,262144]{2,1,0:T(2,128)(2,1)} all-to-all(bf16[4,2,262144]{2,1,0:T(2,128)(2,1)} %reshape.136), channel_id=1, replica_groups=mesh['tile'=8,'member'=4] {'member'}, dimensions={0} | all-to-all | bytes 8388608 | tf_op jit(solution)/shard_map/all_to_all | solution.py:88
  298.5 7.4 %reshape.137 = bf16[512,1,4096]{2,1,0:T(2,128)(2,1)} reshape(bf16[4,2,262144]{2,1,0:T(2,128)(2,1)} %all_to_all.33) | data formatting | bytes 8388608
  305.9 10.1 %copy.60 = bf16[512,1,4096]{2,0,1:T(8,128)(2,1)} copy(bf16[512,1,4096]{2,1,0:T(2,128)(2,1)} %reshape.137) | data formatting | bytes 8388608
  316.1 6.3 %copy.58 = bf16[128,4,1,4096]{0,3,1,2:T(8,128)(2,1)} copy(bf16[128,4,1,4096]{3,0,1,2:T(8,128)(2,1)} %bitcast.75) | data formatting | bytes 8388608 | tf_op jit(solution)/shard_map/all_to_all | solution.py:88
  322.4 6.4 %copy.59 = bf16[128,16384]{1,0:T(8,128)(2,1)} copy(bf16[128,16384]{0,1:T(8,128)(2,1)} %bitcast.77) | data formatting | bytes 8388608 | tf_op jit(solution)/shard_map/reshape | solution.py:89
  (39 shorter events, 12.8 us)
Async XLA Ops:
  0.0 8.1 %copy-start.1 = (s32[4,1024]{1,0:T(4,128)S(1)}, s32[4,1024]{1,0:T(4,128)}, u32[]{:S(2)}) copy-start(s32[4,1024]{1,0:T(4,128)} %param.9) | copy-start | bytes 49156
  4.6 13.3 %collective-permute-start = (bf16[130,1024]{0,1:T(8,128)(2,1)S(1)}, bf16[130,1024]{0,1:T(8,128)(2,1)S(1)}, u32[]{:S(2)}, u32[]{:S(2)}) collective-permute-start(bf16[130,1024]{0,1:T(8,128)(2,1)S(1)} %get-tuple-element.7), channel_id=1, source_target_pairs={{0,4},{4,8},{8,12},{12,16},{16,20},{20,24},{24,28},{28,0},{1,5},{5... | collective-permute-start | bytes 798728 | tf_op jit(solution)/shard_map/ppermute | solution.py:16
  5.1 14.2 %collective-permute-start.1 = (bf16[130,1024]{0,1:T(8,128)(2,1)S(1)}, bf16[130,1024]{0,1:T(8,128)(2,1)S(1)}, u32[]{:S(2)}, u32[]{:S(2)}) collective-permute-start(bf16[130,1024]{0,1:T(8,128)(2,1)S(1)} %get-tuple-element.8), channel_id=1, source_target_pairs={{4,0},{8,4},{12,8},{16,12},{20,16},{24,20},{28,24},{0,28},{5,1},{9... | collective-permute-start | bytes 798728 | tf_op jit(solution)/shard_map/ppermute | solution.py:19
  29.5 1.7 copy-start
  45.1 31.6 %all-to-all-start.1 = ((bf16[128,4,1024]{2,0,1:T(8,128)(2,1)}), bf16[128,4,1024]{2,0,1:T(8,128)(2,1)S(1)}, u32[]{:S(2)}, u32[]{:S(2)}) async-start(bf16[128,4,1024]{2,0,1:T(8,128)(2,1)} %select_bitcast_fusion), calls=%async_computation.1 | async-start | bytes 2097152 | tf_op jit(solution)/shard_map/all_to_all | solution.py:79
  76.7 5.2 %slice-start = ((bf16[130,6144]{0,1:T(8,128)(2,1)}), bf16[2,6144]{0,1:T(8,128)(2,1)S(1)}, s32[]{:S(2)}) async-start(bf16[130,6144]{0,1:T(8,128)(2,1)} %copy-done), calls=%async_computation.3 | async-start | bytes 3145728 | tf_op jit(solution)/shard_map/slice | solution.py:77
  76.7 8.6 %copy-start.2 = (f32[1,1024]{1,0:T(1,128)S(1)}, f32[1,1024]{1,0:T(1,128)}, u32[]{:S(2)}) copy-start(f32[1,1024]{1,0:T(1,128)} %param.10) | copy-start | bytes 12292
  76.7 98.9 %all-to-all-start = ((bf16[128,4,4096]{2,0,1:T(8,128)(2,1)}), bf16[128,4,4096]{2,0,1:T(8,128)(2,1)}, u32[]{:S(2)}, u32[]{:S(2)}) async-start(bf16[128,4,4096]{2,0,1:T(8,128)(2,1)} %bitcast.76), calls=%async_computation | async-start | bytes 8388608 | tf_op jit(solution)/shard_map/all_to_all | solution.py:86
where the time goes:
time: 330 us; the launch traced here: 329 us
  waiting for transfers between devices  114 us (35%)
  blocking collectives  98.7 us (30%)
  local copies, waits for them, and re-layouts  63.7 us (19%)
  other arithmetic  25 us (8%)
  starting transfers between devices  13.6 us (4%)
  matrix products  12.4 us (4%)
    all_to_all x1, blocking collectives, on_device(): lax.all_to_all(updated[:, None, :], 'member', split_axis=0, concat_axis=1...  98.7 us
    all_to_all x1, waiting for transfers between devices, on_device(): lax.all_to_all(state_split, 'member', split_axis=1, concat_axis=0, tiled=...  81.2 us
    unnamed x10, local copies, waits for them, and re-layouts  27.1 us
    all_to_all x1, waiting for transfers between devices, on_device(): lax.all_to_all(picked, 'member', split_axis=1, concat_axis=0, tiled=True)  22 us
    gather x2, local copies, waits for them, and re-layouts, on_device(): picked = jnp.take(obs_pool[:ens_dev], obs_index, axis=1)  12.7 us
    concatenate x1, other arithmetic, with_halo(): block = jnp.concatenate([low, block, high], axis=dim)  10.2 us
    ppermute x1, waiting for transfers between devices, with_halo(): lax.ppermute(lax.slice_in_dim(block, block.shape[dim] - width, None, axis...  9.77 us
    dot_general x10, matrix products, product_f32(): lax.dot_general(left.astype(jnp.float32), right.astype(jnp.float32), (dim...  9.54 us
  transfers between devices with their start and end apart: 4, of which 4 were waited for; matrix products, arithmetic and copies ran while one was open for 5% of the time, Pallas kernels for 0%

commit v1 on v0

--- a/solution.py
+++ b/solution.py
@@ -5,6 +5,29 @@
 
 LOC = 1024
 NS_ITERS = 3
+
+
+def split_up(value, dim, size):
+    before, after = (value.shape[:dim], value.shape[dim + 1 :])
+    return jnp.moveaxis(value.reshape(*before, size, -1, *after), dim, 0)
+
+
+def in_order(blocks, dim):
+    shape = list(blocks.shape[1:])
+    shape[dim] *= blocks.shape[0]
+    return jnp.moveaxis(blocks, 0, dim).reshape(shape)
+
+
+def sent_to_each(x, axis, split_dim, concat_dim):
+    size, here = (lax.axis_size(axis), lax.axis_index(axis))
+    pieces = split_up(x, split_dim, size)
+    out = pieces
+    for step in range(1, size):
+        target, source = ((here + step) % size, (here - step) % size)
+        sent = lax.dynamic_index_in_dim(pieces, target, 0)
+        other = lax.ppermute(sent, axis, [(i, (i + step) % size) for i in range(size)])
+        out = lax.dynamic_update_slice_in_dim(out, other, source, axis=0)
+    return in_order(out, concat_dim)
 
 
 def with_halo(block, sides, width):
@@ -81,10 +104,7 @@
     transform = analysis(obs_block, obs_pair, loc_weight[0])
     group_count = obs_index.shape[0]
     state_split = state.reshape(ens_dev, group_count, state.shape[1] // group_count)
-    updated = transform_state(
-        transform,
-        lax.all_to_all(state_split, "member", split_axis=1, concat_axis=0, tiled=True)[:, 0, :],
-    )
+    updated = transform_state(transform, sent_to_each(state_split, "member", 1, 0)[:, 0, :])
     result = lax.all_to_all(updated[:, None, :], "member", split_axis=0, concat_axis=1, tiled=True)
     return result.reshape(ens_dev, state.shape[1])
 

time: 330 us -> 294 us (0.89)
  waiting for transfers between devices: 114 us -> 51.1 us
  local copies, waits for them, and re-layouts: 63.7 us -> 82.2 us
  blocking collectives: 98.7 us -> 105 us
    all_to_all x1 -> x0, waiting for transfers between devices: 81.2 us -> none  [on_device(): lax.all_to_all(state_split, 'member', split_axis=1, concat_axis=0, tiled=...]
    ppermute x0 -> x3, waiting for transfers between devices: none -> 13.7 us  [sent_to_each(): lax.ppermute(sent, axis, [(i, (i + step) % size) for i in range(size)])]
    ppermute x1, waiting for transfers between devices: 1.46 us -> 12.3 us  [with_halo(): lax.ppermute(lax.slice_in_dim(block, 0, width, axis=dim), axis, backward)]
    ppermute x1, waiting for transfers between devices: 9.77 us -> 1.98 us  [with_halo(): lax.ppermute(lax.slice_in_dim(block, block.shape[dim] - width, None, axis...]
    convert_element_type x0 -> x1, local copies, waits for them, and re-layouts: none -> 7.07 us  [transform_state(): block_f = state_block.astype(jnp.float32)]
    ppermute x0 -> x3, starting transfers between devices: none -> 6.99 us  [sent_to_each(): lax.ppermute(sent, axis, [(i, (i + step) % size) for i in range(size)])]
    dynamic_update_slice x0 -> x3, local copies, waits for them, and re-layouts: none -> 6.79 us  [sent_to_each(): out = lax.dynamic_update_slice_in_dim(out, other, source, axis=0)]
    unnamed x10 -> x19, local copies, waits for them, and re-layouts: 27.1 us -> 33.4 us
  transfers between devices with their start and end apart: 4 -> 6, of which waited for: 4 -> 4; matrix products, arithmetic and copies ran while one was open for 5% -> 18% of each run, Pallas kernels for 0% -> 0%
where the time goes in v1:
time: 294 us; the launch traced here: 293 us
  blocking collectives  105 us (36%)
  local copies, waits for them, and re-layouts  82.2 us (28%)
  waiting for transfers between devices  51.1 us (17%)
  other arithmetic  27.4 us (9%)
  matrix products  14.6 us (5%)
  starting transfers between devices  11.6 us (4%)
    all_to_all x1, blocking collectives, on_device(): lax.all_to_all(updated[:, None, :], 'member', split_axis=0, concat_axis=1...  105 us
    unnamed x19, local copies, waits for them, and re-layouts  33.4 us
    all_to_all x1, waiting for transfers between devices, on_device(): lax.all_to_all(picked, 'member', split_axis=1, concat_axis=0, tiled=True)  23.1 us
    ppermute x3, waiting for transfers between devices, sent_to_each(): lax.ppermute(sent, axis, [(i, (i + step) % size) for i in range(size)])  13.7 us
    gather x2, local copies, waits for them, and re-layouts, on_device(): picked = jnp.take(obs_pool[:ens_dev], obs_index, axis=1)  13.4 us
    ppermute x1, waiting for transfers between devices, with_halo(): lax.ppermute(lax.slice_in_dim(block, 0, width, axis=dim), axis, backward)  12.3 us
    dot_general x10, matrix products, product_f32(): lax.dot_general(left.astype(jnp.float32), right.astype(jnp.float32), (dim...  11.7 us
    concatenate x1, other arithmetic, with_halo(): block = jnp.concatenate([low, block, high], axis=dim)  7.29 us
  transfers between devices with their start and end apart: 6, of which 4 were waited for; matrix products, arithmetic and copies ran while one was open for 18% of the time, Pallas kernels for 0%

profile of v1, /device:TPU:0, one launch (start us, length us, event | category | flops | bytes accessed | tf_op | source)
XLA Modules:
  0.0 292.9 jit_solution(14597237844249492118)
XLA Ops:
  0.0 6.4 %copy.87 = bf16[128,16384]{0,1:T(8,128)(2,1)} copy(bf16[128,16384]{1,0:T(8,128)(2,1)} %param.11) | data formatting | bytes 8388608 | tf_op args[5]
  6.4 3.6 %dynamic-slice_bitcast_fusion = (bf16[1,128,1,4096]{1,3,0,2:T(8,128)(2,1)}, bf16[1,128,1,4096]{1,3,0,2:T(8,128)(2,1)}, bf16[1,128,1,4096]{1,3,0,2:T(8,128)(2,1)}) fusion(bf16[128,4,1,4096]{0,3,1,2:T(8,128)(2,1)} %bitcast.82, s32[]{:T(128)S(6)} %select_n.88, s32[]{:T(128)S(6)} %select_n.84, s32[]{:T(128)S(6)} %select_n.80), kind=kLoop, calls=%fused_computation.36 | loop fusion | bytes 6291468 | tf_op jit(solution)/shard_map/jit(dynamic_index_in_dim)/dynamic_slice | solution.py:27
  10.0 3.1 %collective-permute-start = (bf16[1,128,1,4096]{1,3,0,2:T(8,128)(2,1)}, bf16[1,128,1,4096]{1,3,0,2:T(8,128)(2,1)}, u32[]{:S(2)}, u32[]{:S(2)}) collective-permute-start(bf16[1,128,1,4096]{1,3,0,2:T(8,128)(2,1)} %get-tuple-element.9), channel_id=1, source_target_pairs={{0,1},{1,2},{2,3},{3,0},{4,5},{5,6},{6,7},{7,4},{8,9},{9,10},{10,1... | collective-permute-start | bytes 3145736 | tf_op jit(solution)/shard_map/ppermute | solution.py:28
  13.0 2.6 collective-permute-start.1
  22.3 12.3 %collective-permute-done.4 = bf16[130,1024]{0,1:T(8,128)(2,1)} collective-permute-done((bf16[130,1024]{0,1:T(8,128)(2,1)}, bf16[130,1024]{0,1:T(8,128)(2,1)}, u32[]{:S(2)}, u32[]{:S(2)}) %collective-permute-start.4) | collective-permute-done | bytes 266272 | tf_op jit(solution)/shard_map/ppermute | solution.py:42
  36.7 7.3 %pad_maximum_fusion = bf16[130,6144]{0,1:T(8,128)(2,1)S(1)} fusion(bf16[130,1024]{0,1:T(8,128)(2,1)} %collective-permute-done.4, bf16[1,4096]{0,1:T(8,128)(2,1)S(1)} %broadcast_in_dim.45, bf16[1,4096]{0,1:T(8,128)(2,1)S(1)} %broadcast_in_dim.44, bf16[128,4096]{0,1:T(8,128)(2,1)S(1)} %copy.94, bf16[130,1024]{0,1:T(8,128)(2,1)} %collective-permute-done.3), kind=kLoop, calls=%fused_computation.6 | loop fusion | flops 7987200 | bytes 3194880 | tf_op jit(solution)/shard_map/concatenate | solution.py:43
  45.7 12.1 %gather_fusion = bf16[4096,128]{1,0:T(8,128)(2,1)S(1)} fusion(bf16[128,6144]{0,1:T(8,128)(2,1)S(1)} %slice.28, s32[4096]{0:T(1024)S(1)} %bitcast_clamp_fusion), kind=kCustom, calls=%fused_computation | custom fusion | bytes 2113536 | tf_op jit(solution)/shard_map/jit(_take)/gather | solution.py:101
  59.2 2.4 select_bitcast_fusion
  61.6 3.5 %all-to-all-start = ((bf16[128,4,1024]{2,0,1:T(8,128)(2,1)}), bf16[128,4,1024]{2,0,1:T(8,128)(2,1)S(1)}, u32[]{:S(2)}, u32[]{:S(2)}) async-start(bf16[128,4,1024]{2,0,1:T(8,128)(2,1)} %select_bitcast_fusion), calls=%async_computation | async-start | bytes 2097152 | tf_op jit(solution)/shard_map/all_to_all | solution.py:102
  65.1 3.2 %gather_fusion.1 = bf16[1024,2]{1,0:T(8,128)(2,1)S(1)} fusion(bf16[2,6144]{0,1:T(8,128)(2,1)S(1)} %slice-done, s32[1024]{0:T(1024)S(1)} %broadcast_clamp_fusion), kind=kCustom, calls=%fused_computation.1 | custom fusion | bytes 12288 | tf_op jit(solution)/shard_map/jit(_take)/gather | solution.py:100
  70.8 13.7 %collective-permute-done.1 = bf16[1,128,1,4096]{1,3,0,2:T(8,128)(2,1)} collective-permute-done((bf16[1,128,1,4096]{1,3,0,2:T(8,128)(2,1)}, bf16[1,128,1,4096]{1,3,0,2:T(8,128)(2,1)}, u32[]{:S(2)}, u32[]{:S(2)}) %collective-permute-start.1) | collective-permute-done | bytes 1048608 | tf_op jit(solution)/shard_map/ppermute | solution.py:28
  89.1 2.8 convert_reduce_fusion.1
  91.9 7.1 %copy.99 = f32[4,128,1,4096]{3,1,0,2:T(8,128)} copy(bf16[4,128,1,4096]{1,3,0,2:T(8,128)(2,1)} %constant_dynamic-update-slice_fusion) | data formatting | bytes 12582912 | tf_op jit(solution)/shard_map/convert_element_type | solution.py:87
  99.0 6.4 %fusion = bf16[512,4096]{1,0:T(8,128)(2,1)} fusion(f32[4,128,1,4096]{3,1,0,2:T(8,128)} %copy.99, f32[4096]{0:T(1024)S(1)} %broadcast_multiply_fusion), kind=kLoop, calls=%fused_computation.3 | loop fusion | flops 4194304 | bytes 12599296 | tf_op jit(solution)/shard_map/convert_element_type | solution.py:89
  105.3 23.1 %all-to-all-done = bf16[128,4,1024]{2,0,1:T(8,128)(2,1)S(1)} async-done(((bf16[128,4,1024]{2,0,1:T(8,128)(2,1)}), bf16[128,4,1024]{2,0,1:T(8,128)(2,1)S(1)}, u32[]{:S(2)}, u32[]{:S(2)}) %all-to-all-start) | async-done | bytes 1048608 | tf_op jit(solution)/shard_map/all_to_all | solution.py:102
  128.9 2.3 multiply_reduce_fusion
  139.7 4.6 %fusion.1 = bf16[512,1,4096]{2,0,1:T(8,128)(2,1)} fusion(bf16[512,4096]{1,0:T(8,128)(2,1)S(1)} %copy-done, f32[4096]{0:T(1024)S(1)} %broadcast_multiply_fusion, f32[512,512]{1,0:T(8,128)S(1)} %convolution_divide_fusion, f32[512]{0:T(512)S(1)} %bitcast.89), kind=kOutput, calls=%fused_computation.5 | convolution fusion | flops 2152464384 | bytes 9455616 | tf_op jit(solution)/shard_map/dot_general | solution.py:48
  144.8 6.7 %reduce.4 = bf16[512,4096]{1,0:T(8,128)(2,1)} reduce(bf16[512,1,4096]{2,0,1:T(8,128)(2,1)} %fusion.1, bf16[]{:T(256)} %broadcast.132), dimensions={1}, to_apply=%copy.100.reduce_sub_computation | reduce | bytes 8388610 | tf_op jit(solution)/shard_map/broadcast_in_dim | solution.py:108
  151.5 6.2 %reshape.130 = bf16[4,2,262144]{2,1,0:T(2,128)(2,1)} reshape(bf16[512,4096]{1,0:T(8,128)(2,1)} %reduce.4) | data formatting | bytes 8388608
  157.7 104.9 %all_to_all.24 = bf16[4,2,262144]{2,1,0:T(2,128)(2,1)} all-to-all(bf16[4,2,262144]{2,1,0:T(2,128)(2,1)} %reshape.130), channel_id=1, replica_groups=mesh['tile'=8,'member'=4] {'member'}, dimensions={0} | all-to-all | bytes 8388608 | tf_op jit(solution)/shard_map/all_to_all | solution.py:108
  262.7 7.4 %reshape.131 = bf16[512,1,4096]{2,1,0:T(2,128)(2,1)} reshape(bf16[4,2,262144]{2,1,0:T(2,128)(2,1)} %all_to_all.24) | data formatting | bytes 8388608
  270.1 10.1 %copy.109 = bf16[512,1,4096]{2,0,1:T(8,128)(2,1)} copy(bf16[512,1,4096]{2,1,0:T(2,128)(2,1)} %reshape.131) | data formatting | bytes 8388608
  280.2 6.3 %copy.101 = bf16[128,4,1,4096]{0,3,1,2:T(8,128)(2,1)} copy(bf16[128,4,1,4096]{3,0,1,2:T(8,128)(2,1)} %bitcast.84) | data formatting | bytes 8388608 | tf_op jit(solution)/shard_map/all_to_all | solution.py:108
  286.6 6.4 %copy.102 = bf16[128,16384]{1,0:T(8,128)(2,1)} copy(bf16[128,16384]{0,1:T(8,128)(2,1)} %bitcast.85) | data formatting | bytes 8388608 | tf_op jit(solution)/shard_map/reshape | solution.py:109
  (56 shorter events, 27.3 us)
Async XLA Ops:
  6.4 10.6 %copy-start.3 = (bf16[4096]{0:T(1024)(128)(2,1)S(1)}, bf16[4096]{0:T(1024)(128)(2,1)}, u32[]{:S(2)}) copy-start(bf16[4096]{0:T(1024)(128)(2,1)} %param.8) | copy-start | bytes 24580
  6.4 11.2 %copy-start.4 = (bf16[4096]{0:T(1024)(128)(2,1)S(1)}, bf16[4096]{0:T(1024)(128)(2,1)}, u32[]{:S(2)}) copy-start(bf16[4096]{0:T(1024)(128)(2,1)} %param.7) | copy-start | bytes 24580
  10.0 58.5 %collective-permute-start = (bf16[1,128,1,4096]{1,3,0,2:T(8,128)(2,1)}, bf16[1,128,1,4096]{1,3,0,2:T(8,128)(2,1)}, u32[]{:S(2)}, u32[]{:S(2)}) collective-permute-start(bf16[1,128,1,4096]{1,3,0,2:T(8,128)(2,1)} %get-tuple-element.9), channel_id=1, source_target_pairs={{0,1},{1,2},{2,3},{3,0},{4,5},{5,6},{6,7},{7,4},{8,9},{9,10},{10,1... | collective-permute-start | bytes 3145736 | tf_op jit(solution)/shard_map/ppermute | solution.py:28
  13.0 71.5 %collective-permute-start.1 = (bf16[1,128,1,4096]{1,3,0,2:T(8,128)(2,1)}, bf16[1,128,1,4096]{1,3,0,2:T(8,128)(2,1)}, u32[]{:S(2)}, u32[]{:S(2)}) collective-permute-start(bf16[1,128,1,4096]{1,3,0,2:T(8,128)(2,1)} %get-tuple-element.8), channel_id=1, source_target_pairs={{0,2},{1,3},{2,0},{3,1},{4,6},{5,7},{6,4},{7,5},{8,10},{9,11},{10,... | collective-permute-start | bytes 3145736 | tf_op jit(solution)/shard_map/ppermute | solution.py:28
  15.6 6.6 %copy-start.2 = (s32[4,1024]{1,0:T(4,128)S(1)}, s32[4,1024]{1,0:T(4,128)}, u32[]{:S(2)}) copy-start(s32[4,1024]{1,0:T(4,128)} %param.9) | copy-start | bytes 49156
  15.6 71.2 %collective-permute-start.2 = (bf16[1,128,1,4096]{1,3,0,2:T(8,128)(2,1)}, bf16[1,128,1,4096]{1,3,0,2:T(8,128)(2,1)}, u32[]{:S(2)}, u32[]{:S(2)}) collective-permute-start(bf16[1,128,1,4096]{1,3,0,2:T(8,128)(2,1)} %get-tuple-element.7), channel_id=1, source_target_pairs={{0,3},{1,0},{2,1},{3,2},{4,7},{5,4},{6,5},{7,6},{8,11},{9,8},{10,9... | collective-permute-start | bytes 3145736 | tf_op jit(solution)/shard_map/ppermute | solution.py:28
  21.1 13.6 %collective-permute-start.4 = (bf16[130,1024]{0,1:T(8,128)(2,1)}, bf16[130,1024]{0,1:T(8,128)(2,1)}, u32[]{:S(2)}, u32[]{:S(2)}) collective-permute-start(bf16[130,1024]{0,1:T(8,128)(2,1)} %get-tuple-element.11), channel_id=1, source_target_pairs={{4,0},{8,4},{12,8},{16,12},{20,16},{24,20},{28,24},{0,28},{5,1},{9... | collective-permute-start | bytes 798728 | tf_op jit(solution)/shard_map/ppermute | solution.py:42
  22.2 14.5 %collective-permute-start.3 = (bf16[130,1024]{0,1:T(8,128)(2,1)}, bf16[130,1024]{0,1:T(8,128)(2,1)}, u32[]{:S(2)}, u32[]{:S(2)}) collective-permute-start(bf16[130,1024]{0,1:T(8,128)(2,1)} %get-tuple-element.10), channel_id=1, source_target_pairs={{0,4},{4,8},{8,12},{12,16},{16,20},{20,24},{24,28},{28,0},{1,5},{5... | collective-permute-start | bytes 798728 | tf_op jit(solution)/shard_map/ppermute | solution.py:39
  44.0 1.6 copy-start.1
  59.2 5.9 %slice-start = ((bf16[130,6144]{0,1:T(8,128)(2,1)}), bf16[2,6144]{0,1:T(8,128)(2,1)S(1)}, s32[]{:S(2)}) async-start(bf16[130,6144]{0,1:T(8,128)(2,1)} %copy-done.1), calls=%async_computation.2 | async-start | bytes 3145728 | tf_op jit(solution)/shard_map/slice | solution.py:100
  59.2 9.3 %copy-start.5 = (f32[1,1024]{1,0:T(1,128)S(1)}, f32[1,1024]{1,0:T(1,128)}, u32[]{:S(2)}) copy-start(f32[1,1024]{1,0:T(1,128)} %param.10) | copy-start | bytes 12292
  61.6 66.8 %all-to-all-start = ((bf16[128,4,1024]{2,0,1:T(8,128)(2,1)}), bf16[128,4,1024]{2,0,1:T(8,128)(2,1)S(1)}, u32[]{:S(2)}, u32[]{:S(2)}) async-start(bf16[128,4,1024]{2,0,1:T(8,128)(2,1)} %select_bitcast_fusion), calls=%async_computation | async-start | bytes 2097152 | tf_op jit(solution)/shard_map/all_to_all | solution.py:102
  131.9 2.2 copy-start.6
  136.8 2.9 copy-start
